TPU v7x, 32 devices: a whole 2x2x4 slice. The times are simulated.
32 devices in a mesh: gx: 4 (over z), gy: 2 (over core), gz: 4 (over y, x).
Axes of the slice: x: 2, y: 2, z: 4, core: 2. Of those that a mesh axis runs over, the one named last changes fastest.
Arguments:
- density: float32 [64, 64, 256], P('gz', 'gx', 'gy'), may hold values from -8 to 8
Outputs:
- potential: float32 [64, 64, 256], P('gz', 'gx', 'gy')
- forces: float32 [3, 64, 64, 256], P(None, 'gz', 'gx', 'gy')
All inputs are finite; a program needn't handle non-finite values.
Results may differ from a plain program's by a relative error of at most 0.0003.
Values sent between devices are 32-bit elements; how exact they have to be, the bound alone decides.
A program may use at most 64 MiB of HBM per device.

v0:
```python
import jax
import jax.numpy as jnp
from jax import lax
from jax.sharding import PartitionSpec as P

RADIUS = 15
MARGIN = 16
SCREEN = 32


PRECISE = lax.Precision.HIGHEST
WEIGHTS = (1.0, 0.7, 0.5)
FRACTIONS = (0.5, 0.25, 0.125)
AMPLITUDE = 2.0
SMOOTHING = 1.0
TWO_PI = 6.283185307179586


def extended_2(cells, sides, width):
    for axis, dim in sides:
        count = lax.axis_size(axis)
        head = lax.slice_in_dim(cells, 0, width, axis=dim)
        tail = lax.slice_in_dim(cells, cells.shape[dim] - width, cells.shape[dim], axis=dim)
        cells = jnp.concatenate(
            [
                lax.ppermute(tail, axis, [(i, (i + 1) % count) for i in range(count)]),
                cells,
                lax.ppermute(head, axis, [((i + 1) % count, i) for i in range(count)]),
            ],
            axis=dim,
        )
    return cells


def profile(offset, spread):
    offsets = jnp.arange(-RADIUS, RADIUS + 1).astype(jnp.float32)
    norm_sum = jnp.sqrt(jnp.sum(jnp.exp(-offsets * offsets / (spread * spread))))
    inside = jnp.abs(offset) <= RADIUS
    return jnp.where(inside, jnp.exp(-offset * offset / (2.0 * spread * spread)), 0.0) / norm_sum


def band_pair(length, spread):
    rows_out = jnp.arange(length).astype(jnp.float32)[:, None]
    rows_in = jnp.arange(length + 2 * MARGIN).astype(jnp.float32)[None, :]
    offset = rows_out + MARGIN - rows_in
    smooth = profile(offset, spread)
    slope_part = -0.5 * (profile(offset + 1.0, spread) - profile(offset - 1.0, spread))
    return (smooth, slope_part)


def short_range(padded, size_x, size_y, size_z):
    mats_x = []
    mats_y = []
    mats_z = []
    for fraction, weight in zip(FRACTIONS, WEIGHTS):
        spread = RADIUS * fraction
        mats_x.append(jnp.stack(band_pair(size_x, spread)))
        mats_y.append(jnp.stack(band_pair(size_y, spread)))
        smooth_z, slope_z = band_pair(size_z, spread)
        mats_z.append(jnp.stack([weight * smooth_z, weight * slope_z]))
    stack_x = jnp.stack(mats_x)
    stack_y = jnp.stack(mats_y)
    stack_z = jnp.stack(mats_z)
    section_one = jnp.einsum("gsia,abc->gsibc", stack_x, padded, precision=PRECISE)
    section_two = jnp.einsum("gtjb,gibc->gtijc", stack_y, section_one[:, 0], precision=PRECISE)
    section_three = jnp.einsum(
        "gjb,gibc->gijc", stack_y[:, 0], section_one[:, 1], precision=PRECISE
    )
    smooth_pair = jnp.einsum("gijc,gtkc->tijk", section_two[:, 0], stack_z, precision=PRECISE)
    near_y = jnp.einsum("gijc,gkc->ijk", section_two[:, 1], stack_z[:, 0], precision=PRECISE)
    near_x = jnp.einsum("gijc,gkc->ijk", section_three, stack_z[:, 0], precision=PRECISE)
    return (smooth_pair[0], near_x, near_y, smooth_pair[1])


def unit_phase(product, modulus):
    angles = TWO_PI * (product % modulus).astype(jnp.float32) / modulus
    return (jnp.cos(angles), jnp.sin(angles))


def symbol(indices, length):
    angles = jnp.pi * indices.astype(jnp.float32) / length
    return (4.0 * jnp.sin(angles) ** 2, indices == length // 2, indices == 0)


def rotate(pattern, cos_t, sin_t, real_part, imag_part, direction):
    real_out = jnp.einsum(pattern, cos_t, real_part, precision=PRECISE) - direction * jnp.einsum(
        pattern, sin_t, imag_part, precision=PRECISE
    )
    imag_out = direction * jnp.einsum(pattern, sin_t, real_part, precision=PRECISE) + jnp.einsum(
        pattern, cos_t, imag_part, precision=PRECISE
    )
    return (real_out, imag_out)


def swap_rows(payload):
    return lax.all_to_all(payload, "gx", split_axis=2, concat_axis=2, tiled=True)


def swap_depth(payload):
    return lax.all_to_all(payload, "gz", split_axis=2, concat_axis=2, tiled=True)


def swap_columns(payload):
    return lax.all_to_all(payload, ("gx", "gy"), split_axis=2, concat_axis=2, tiled=True)


def long_range(density):
    size_x, size_y, size_z = density.shape
    count_gx = lax.axis_size("gx")
    count_gy = lax.axis_size("gy")
    count_gz = lax.axis_size("gz")
    local_x = size_x // 2
    local_y = size_y // 2
    local_z = size_z // 2
    depth_z = local_z // count_gx
    total_x = local_x * count_gz
    total_y = local_y * count_gx
    total_z = local_z * count_gy
    groups = count_gx * count_gy
    block_x = total_x // groups
    block_y = total_y // count_gz
    own_group = lax.axis_index("gx") * count_gy + lax.axis_index("gy")
    own_depth = lax.axis_index("gz")
    coarse = density.reshape(local_x, 2, local_y, 2, local_z, 2).mean(axis=(1, 3, 5))
    freq_y = jnp.arange(count_gz)[:, None] * block_y + jnp.arange(block_y)[None, :]
    pos_y = jnp.arange(count_gx)[:, None] * local_y + jnp.arange(local_y)[None, :]
    cos_y, sin_y = unit_phase(freq_y[:, :, None, None] * pos_y[None, None, :, :], total_y)
    rows_in = swap_rows(coarse.reshape(local_x, local_y, count_gx, depth_z))
    real_y = jnp.einsum("qrab,xbal->xqrl", cos_y, rows_in, precision=PRECISE)
    imag_y = -jnp.einsum("qrab,xbal->xqrl", sin_y, rows_in, precision=PRECISE)
    depth_in = swap_depth(jnp.stack([real_y, imag_y]))
    freq_x = jnp.arange(groups)[:, None] * block_x + jnp.arange(block_x)[None, :]
    pos_x = jnp.arange(count_gz)[:, None] * local_x + jnp.arange(local_x)[None, :]
    cos_x, sin_x = unit_phase(freq_x[:, :, None, None] * pos_x[None, None, :, :], total_x)
    real_x, imag_x = rotate("pscx,xcrl->sprl", cos_x, sin_x, depth_in[0], depth_in[1], -1.0)
    cols_in = swap_columns(jnp.stack([real_x, imag_x]))
    source = jnp.arange(groups)
    pos_z = (source % count_gy * local_z + source // count_gy * depth_z)[:, None] + jnp.arange(
        depth_z
    )[None, :]
    cos_z, sin_z = unit_phase(jnp.arange(total_z)[:, None, None] * pos_z[None, :, :], total_z)
    real_z, imag_z = rotate("kjl,sjrl->srk", cos_z, sin_z, cols_in[0], cols_in[1], -1.0)
    wave_x, edge_x, zero_x = symbol(own_group * block_x + jnp.arange(block_x), total_x)
    wave_y, edge_y, zero_y = symbol(own_depth * block_y + jnp.arange(block_y), total_y)
    wave_z, edge_z, zero_z = symbol(jnp.arange(total_z), total_z)
    kappa_sq = wave_x[:, None, None] + wave_y[None, :, None] + wave_z[None, None, :]
    dropped = edge_x[:, None, None] | edge_y[None, :, None] | edge_z[None, None, :]
    dropped = dropped | zero_x[:, None, None] & zero_y[None, :, None] & zero_z[None, None, :]
    green_fn = jnp.where(
        dropped,
        0.0,
        AMPLITUDE
        * jnp.exp(-SMOOTHING * SMOOTHING * kappa_sq)
        / (kappa_sq + 1.0 / (SCREEN * SCREEN)),
    )
    real_g = real_z * green_fn
    imag_g = imag_z * green_fn
    back_real, back_imag = rotate("kjl,srk->sjrl", cos_z, sin_z, real_g, imag_g, 1.0)
    cols_out = swap_columns(jnp.stack([back_real, back_imag]))
    real_b, imag_b = rotate("pscx,sprl->xcrl", cos_x, sin_x, cols_out[0], cols_out[1], 1.0)
    depth_out = swap_depth(jnp.stack([real_b, imag_b]))
    scale_y = jnp.ones(freq_y.shape, jnp.float32)
    result = jnp.einsum(
        "qrab,xqrl->xbal", cos_y * scale_y[:, :, None, None], depth_out[0], precision=PRECISE
    )
    result = result - jnp.einsum(
        "qrab,xqrl->xbal", sin_y * scale_y[:, :, None, None], depth_out[1], precision=PRECISE
    )
    result = result / (total_x * total_y * total_z)
    rows_out = swap_rows(result)
    return rows_out.reshape(local_x, local_y, local_z)


def transfer_pair(length):
    fine_cells = jnp.arange(-1, length + 1)
    parent = jnp.floor_divide(fine_cells, 2)
    parity = fine_cells - 2 * parent
    neighbour = parent - 1 + 2 * parity
    coarse_slots = jnp.arange(length // 2 + 2) - 1
    extended = 0.75 * (coarse_slots[None, :] == parent[:, None]).astype(jnp.float32)
    extended = extended + 0.25 * (coarse_slots[None, :] == neighbour[:, None]).astype(jnp.float32)
    value_map = extended[1 : length + 1]
    slope_map = -0.5 * (extended[2:] - extended[:-2])
    return (value_map, slope_map)


def prolong_brick(coarse_rims, size_x, size_y, size_z):
    value_x, slope_x = transfer_pair(size_x)
    value_y, slope_y = transfer_pair(size_y)
    value_z, slope_z = transfer_pair(size_z)
    along_z = jnp.einsum(
        "abe,tze->tabz", coarse_rims, jnp.stack([value_z, slope_z]), precision=PRECISE
    )
    level_y = jnp.einsum("aez,ye->ayz", along_z[0], value_y, precision=PRECISE)
    cross_y = jnp.einsum("aez,ye->ayz", along_z[0], slope_y, precision=PRECISE)
    cross_z = jnp.einsum("aez,ye->ayz", along_z[1], value_y, precision=PRECISE)
    far_pot = jnp.einsum("ayz,xa->xyz", level_y, value_x, precision=PRECISE)
    far_x = jnp.einsum("ayz,xa->xyz", level_y, slope_x, precision=PRECISE)
    far_y = jnp.einsum("ayz,xa->xyz", cross_y, value_x, precision=PRECISE)
    far_z = jnp.einsum("ayz,xa->xyz", cross_z, value_x, precision=PRECISE)
    return (far_pot, far_x, far_y, far_z)


def shards(density):
    size_x, size_y, size_z = density.shape
    padded = extended_2(density, (("gx", 1), ("gy", 2), ("gz", 0)), MARGIN)
    coarse_field = long_range(density)
    near_pot, near_x, near_y, near_z = short_range(padded, size_x, size_y, size_z)
    coarse_rims = extended_2(coarse_field, (("gx", 1), ("gy", 2), ("gz", 0)), 1)
    far_pot, far_x, far_y, far_z = prolong_brick(coarse_rims, size_x, size_y, size_z)
    potential = near_pot + far_pot
    forces = jnp.stack([near_x + far_x, near_y + far_y, near_z + far_z])
    return (potential, forces)


def solution(mesh):
    return jax.shard_map(
        shards,
        mesh=mesh,
        in_specs=(P("gz", "gx", "gy"),),
        out_specs=(P("gz", "gx", "gy"), P(None, "gz", "gx", "gy")),
        check_vma=False,
    )
```

profile of v0, /device:TPU:0, one launch (start us, length us, event | category | flops | bytes accessed | tf_op | source)
XLA Modules:
  0.0 160.6 jit_solution(10579443121876831432)
XLA Ops:
  0.6 1.0 copy.75
  1.6 3.1 %collective-permute-start = (f32[16,16,128]{2,0,1:T(8,128)S(1)}, f32[16,16,128]{2,0,1:T(8,128)S(1)}, u32[]{:S(2)}, u32[]{:S(2)}) collective-permute-start(f32[16,16,128]{2,0,1:T(8,128)S(1)} %copy.75), channel_id=1, source_target_pairs={{0,8},{8,16},{16,24},{24,0},{1,9},{9,17},{17,25},{25,1},{2,10},{10... | collective-permute-start | bytes 393224 | tf_op jit(solution)/shard_map/ppermute | solution.py:26
  4.7 2.1 %collective-permute-start.1 = (f32[16,16,128]{2,0,1:T(8,128)S(1)}, f32[16,16,128]{2,0,1:T(8,128)S(1)}, u32[]{:S(2)}, u32[]{:S(2)}) collective-permute-start(f32[16,16,128]{2,0,1:T(8,128)S(1)} %copy.75), channel_id=1, source_target_pairs={{8,0},{16,8},{24,16},{0,24},{9,1},{17,9},{25,17},{1,25},{10,2},{18... | collective-permute-start | bytes 393224 | tf_op jit(solution)/shard_map/ppermute | solution.py:28
  6.8 10.5 %reshape.1175 = f32[8,2,8,2,64,2]{5,4,3,2,1,0:T(8,128)} reshape(f32[16,16,128]{2,1,0:T(8,128)} %param.1) | data formatting | bytes 262144 | tf_op jit(solution)/shard_map/reshape | solution.py:124
  17.3 4.0 %reduce_sum.41 = f32[8,8,64]{2,1,0:T(8,128)S(1)} reduce(f32[8,2,8,2,64,2]{5,4,3,2,1,0:T(8,128)} %reshape.1175, f32[]{:T(128)} %constant.203.clone.1), dimensions={1,3,5}, to_apply=%region_3.4 | reduce | flops 28672 | bytes 147460 | tf_op jit(solution)/shard_map/reduce_sum | solution.py:124
  22.2 3.3 %all-to-all-start = ((f32[4,1,1024]{2,1,0:T(1,128)}), f32[4,1,1024]{2,1,0:T(1,128)S(1)}, u32[]{:S(2)}, u32[]{:S(2)}) async-start(f32[4,1,1024]{2,1,0:T(1,128)} %reshape.1229), calls=%async_computation | async-start | bytes 32768 | tf_op jit(solution)/shard_map/all_to_all | solution.py:96
  33.7 3.9 %all-to-all-start.1 = ((f32[4,1,2048]{2,1,0:T(1,128)}), f32[4,1,2048]{2,1,0:T(1,128)S(1)}, u32[]{:S(2)}, u32[]{:S(2)}) async-start(f32[4,1,2048]{2,1,0:T(1,128)} %reshape.1231), calls=%async_computation.1 | async-start | bytes 65536 | tf_op jit(solution)/shard_map/all_to_all | solution.py:100
  37.6 4.8 %all-to-all-done.1 = f32[4,1,2048]{2,1,0:T(1,128)S(1)} async-done(((f32[4,1,2048]{2,1,0:T(1,128)}), f32[4,1,2048]{2,1,0:T(1,128)S(1)}, u32[]{:S(2)}, u32[]{:S(2)}) %all-to-all-start.1) | async-done | bytes 32800 | tf_op jit(solution)/shard_map/all_to_all | solution.py:100
  46.7 5.0 %all-to-all-start.2 = ((f32[8,1,1024]{2,1,0:T(1,128)}), f32[8,1,1024]{2,1,0:T(1,128)S(1)}, u32[]{:S(2)}, u32[]{:S(2)}) async-start(f32[8,1,1024]{2,1,0:T(1,128)} %reshape.1233), calls=%async_computation.2 | async-start | bytes 65536 | tf_op jit(solution)/shard_map/all_to_all | solution.py:104
  51.7 5.7 %all-to-all-done.2 = f32[8,1,1024]{2,1,0:T(1,128)S(1)} async-done(((f32[8,1,1024]{2,1,0:T(1,128)}), f32[8,1,1024]{2,1,0:T(1,128)S(1)}, u32[]{:S(2)}, u32[]{:S(2)}) %all-to-all-start.2) | async-done | bytes 32800 | tf_op jit(solution)/shard_map/all_to_all | solution.py:104
  61.0 0.8 fusion.152
  62.4 0.8 fusion.22
  63.2 0.8 fusion.21
  64.9 3.5 %all-to-all-start.3 = ((f32[8,1,1024]{2,1,0:T(1,128)}), f32[8,1,1024]{2,1,0:T(1,128)S(1)}, u32[]{:S(2)}, u32[]{:S(2)}) async-start(f32[8,1,1024]{2,1,0:T(1,128)} %reshape.1235), calls=%async_computation.3 | async-start | bytes 65536 | tf_op jit(solution)/shard_map/all_to_all | solution.py:104
  68.4 5.5 %all-to-all-done.3 = f32[8,1,1024]{2,1,0:T(1,128)S(1)} async-done(((f32[8,1,1024]{2,1,0:T(1,128)}), f32[8,1,1024]{2,1,0:T(1,128)S(1)}, u32[]{:S(2)}, u32[]{:S(2)}) %all-to-all-start.3) | async-done | bytes 32800 | tf_op jit(solution)/shard_map/all_to_all | solution.py:104
  78.0 3.3 %all-to-all-start.4 = ((f32[4,1,2048]{2,1,0:T(1,128)}), f32[4,1,2048]{2,1,0:T(1,128)S(1)}, u32[]{:S(2)}, u32[]{:S(2)}) async-start(f32[4,1,2048]{2,1,0:T(1,128)} %reshape.1237), calls=%async_computation.4 | async-start | bytes 65536 | tf_op jit(solution)/shard_map/all_to_all | solution.py:100
  81.3 4.7 %all-to-all-done.4 = f32[4,1,2048]{2,1,0:T(1,128)S(1)} async-done(((f32[4,1,2048]{2,1,0:T(1,128)}), f32[4,1,2048]{2,1,0:T(1,128)S(1)}, u32[]{:S(2)}, u32[]{:S(2)}) %all-to-all-start.4) | async-done | bytes 32800 | tf_op jit(solution)/shard_map/all_to_all | solution.py:100
  88.9 3.3 %all-to-all-start.5 = ((f32[4,1,1024]{2,1,0:T(1,128)}), f32[4,1,1024]{2,1,0:T(1,128)S(1)}, u32[]{:S(2)}, u32[]{:S(2)}) async-start(f32[4,1,1024]{2,1,0:T(1,128)} %reshape.1239), calls=%async_computation.5 | async-start | bytes 32768 | tf_op jit(solution)/shard_map/all_to_all | solution.py:96
  92.2 5.5 %all-to-all-done.5 = f32[4,1,1024]{2,1,0:T(1,128)S(1)} async-done(((f32[4,1,1024]{2,1,0:T(1,128)}), f32[4,1,1024]{2,1,0:T(1,128)S(1)}, u32[]{:S(2)}, u32[]{:S(2)}) %all-to-all-start.5) | async-done | bytes 16416 | tf_op jit(solution)/shard_map/all_to_all | solution.py:96
  99.4 3.2 %collective-permute-start.7 = (f32[8,1,64]{2,1,0:T(1,128)S(1)}, f32[8,1,64]{2,1,0:T(1,128)S(1)}, u32[]{:S(2)}, u32[]{:S(2)}) collective-permute-start(f32[8,1,64]{2,1,0:T(1,128)S(1)} %get-tuple-element.23), channel_id=1, source_target_pairs={{8,0},{16,8},{24,16},{0,24},{9,1},{17,9},{25,17},{1,25},{10,2},{18... | collective-permute-start | bytes 6152 | tf_op jit(solution)/shard_map/ppermute | solution.py:28
  102.6 1.6 collective-permute-done.6
  106.5 2.3 %collective-permute-start.11 = (f32[1,10,66]{2,1,0:T(8,128)S(1)}, f32[1,10,66]{2,1,0:T(8,128)S(1)}, u32[]{:S(2)}, u32[]{:S(2)}) collective-permute-start(f32[1,10,66]{2,1,0:T(8,128)S(1)} %get-tuple-element.17), channel_id=1, source_target_pairs={{1,0},{2,1},{3,2},{0,3},{5,4},{6,5},{7,6},{4,7},{9,8},{10,9},{11,1... | collective-permute-start | bytes 7928 | tf_op jit(solution)/shard_map/ppermute | solution.py:28
  109.2 2.9 %collective-permute-start.5 = (f32[16,48,160]{2,0,1:T(8,128)S(1)}, f32[16,48,160]{2,0,1:T(8,128)S(1)}, u32[]{:S(2)}, u32[]{:S(2)}) collective-permute-start(f32[16,48,160]{2,0,1:T(8,128)S(1)} %pad_maximum_fusion), channel_id=1, source_target_pairs={{1,0},{2,1},{3,2},{0,3},{5,4},{6,5},{7,6},{4,7},{9,8},{10,9},{11,1... | collective-permute-start | bytes 1474568 | tf_op jit(solution)/shard_map/ppermute | solution.py:28
  114.2 16.3 %collective-permute-done.4 = f32[16,48,160]{2,0,1:T(8,128)S(1)} collective-permute-done((f32[16,48,160]{2,0,1:T(8,128)S(1)}, f32[16,48,160]{2,0,1:T(8,128)S(1)}, u32[]{:S(2)}, u32[]{:S(2)}) %collective-permute-start.4) | collective-permute-done | bytes 491552 | tf_op jit(solution)/shard_map/ppermute | solution.py:26
  130.5 14.9 %collective-permute-done.5 = f32[16,48,160]{2,0,1:T(8,128)S(1)} collective-permute-done((f32[16,48,160]{2,0,1:T(8,128)S(1)}, f32[16,48,160]{2,0,1:T(8,128)S(1)}, u32[]{:S(2)}, u32[]{:S(2)}) %collective-permute-start.5) | collective-permute-done | bytes 491552 | tf_op jit(solution)/shard_map/ppermute | solution.py:28
  145.4 4.0 %fusion = f32[3,2,16,48,160]{4,2,3,1,0:T(8,128)S(1)} fusion(f32[16,48,160]{2,0,1:T(8,128)S(1)} %collective-permute-done.5, f32[16,48,16]{2,0,1:T(8,128)S(1)} %collective-permute-done.3, f32[16,48,128]{2,0,1:T(8,128)S(1)} %constant_dynamic-update-slice_fusion, f32[16,48,16]{2,0,1:T(8,128)S(1)} %collective-permute-done.2, ...), kind=kOutput, calls=%fused_computation.3 | convolution fusion | flops 426157056 | bytes 4442112 | tf_op jit(solution)/shard_map/gsia,abc->gsibc/dot_general | solution.py:64
  149.4 1.0 slice_bitcast_fusion
  150.4 3.0 %fusion.13 = f32[3,2,16,16,160]{4,3,1,2,0:T(8,128)S(1)} fusion(f32[3,16,48,160,1]{3,1,2,0,4:T(8,128)S(1)} %get-tuple-element.3, f32[1,2,16,48]{3,2,1,0:T(8,128)S(1)} %maximum_bitcast_fusion.11, f32[1,2,16,48]{3,2,1,0:T(8,128)S(1)} %get-tuple-element.39, f32[1,2,16,48]{3,2,1,0:T(8,128)S(1)} %get-tuple-element.38), kind=kOutput, calls=%fused_computation.16 | convolution fusion | flops 141566976 | bytes 2476032 | tf_op jit(solution)/shard_map/gtjb,gibc->gtijc/dot_general | solution.py:65
  153.4 1.0 convolution_bitcast_fusion
  154.5 2.9 %fusion.16 = f32[3,16,16,160]{3,2,0,1:T(8,128)S(1)} fusion(f32[3,16,48,160]{3,1,2,0:T(8,128)S(1)} %get-tuple-element.2, f32[3,2,16,48]{3,2,1,0:T(8,128)S(1)} %pad_maximum_fusion.8), kind=kOutput, calls=%fused_computation.17 | convolution fusion | flops 70778880 | bytes 2875392 | tf_op jit(solution)/shard_map/gjb,gibc->gijc/dot_general | solution.py:66
  157.4 0.8 fusion.39
  158.2 0.8 fusion.37
  (127 shorter events, 31.1 us)
Async XLA Ops:
  1.6 79.7 %collective-permute-start = (f32[16,16,128]{2,0,1:T(8,128)S(1)}, f32[16,16,128]{2,0,1:T(8,128)S(1)}, u32[]{:S(2)}, u32[]{:S(2)}) collective-permute-start(f32[16,16,128]{2,0,1:T(8,128)S(1)} %copy.75), channel_id=1, source_target_pairs={{0,8},{8,16},{16,24},{24,0},{1,9},{9,17},{17,25},{25,1},{2,10},{10... | collective-permute-start | bytes 393224 | tf_op jit(solution)/shard_map/ppermute | solution.py:26
  4.7 97.9 %collective-permute-start.1 = (f32[16,16,128]{2,0,1:T(8,128)S(1)}, f32[16,16,128]{2,0,1:T(8,128)S(1)}, u32[]{:S(2)}, u32[]{:S(2)}) collective-permute-start(f32[16,16,128]{2,0,1:T(8,128)S(1)} %copy.75), channel_id=1, source_target_pairs={{8,0},{16,8},{24,16},{0,24},{9,1},{17,9},{25,17},{1,25},{10,2},{18... | collective-permute-start | bytes 393224 | tf_op jit(solution)/shard_map/ppermute | solution.py:28
  22.2 8.8 %all-to-all-start = ((f32[4,1,1024]{2,1,0:T(1,128)}), f32[4,1,1024]{2,1,0:T(1,128)S(1)}, u32[]{:S(2)}, u32[]{:S(2)}) async-start(f32[4,1,1024]{2,1,0:T(1,128)} %reshape.1229), calls=%async_computation | async-start | bytes 32768 | tf_op jit(solution)/shard_map/all_to_all | solution.py:96
  33.7 8.6 %all-to-all-start.1 = ((f32[4,1,2048]{2,1,0:T(1,128)}), f32[4,1,2048]{2,1,0:T(1,128)S(1)}, u32[]{:S(2)}, u32[]{:S(2)}) async-start(f32[4,1,2048]{2,1,0:T(1,128)} %reshape.1231), calls=%async_computation.1 | async-start | bytes 65536 | tf_op jit(solution)/shard_map/all_to_all | solution.py:100
  46.7 10.7 %all-to-all-start.2 = ((f32[8,1,1024]{2,1,0:T(1,128)}), f32[8,1,1024]{2,1,0:T(1,128)S(1)}, u32[]{:S(2)}, u32[]{:S(2)}) async-start(f32[8,1,1024]{2,1,0:T(1,128)} %reshape.1233), calls=%async_computation.2 | async-start | bytes 65536 | tf_op jit(solution)/shard_map/all_to_all | solution.py:104
  64.9 9.0 %all-to-all-start.3 = ((f32[8,1,1024]{2,1,0:T(1,128)}), f32[8,1,1024]{2,1,0:T(1,128)S(1)}, u32[]{:S(2)}, u32[]{:S(2)}) async-start(f32[8,1,1024]{2,1,0:T(1,128)} %reshape.1235), calls=%async_computation.3 | async-start | bytes 65536 | tf_op jit(solution)/shard_map/all_to_all | solution.py:104
  75.4 16.7 %copy-start = (f32[16,16,128]{2,1,0:T(8,128)S(1)}, f32[16,16,128]{2,1,0:T(8,128)}, u32[]{:S(2)}) copy-start(f32[16,16,128]{2,1,0:T(8,128)} %param.1) | copy-start | bytes 393220
  78.0 8.0 %all-to-all-start.4 = ((f32[4,1,2048]{2,1,0:T(1,128)}), f32[4,1,2048]{2,1,0:T(1,128)S(1)}, u32[]{:S(2)}, u32[]{:S(2)}) async-start(f32[4,1,2048]{2,1,0:T(1,128)} %reshape.1237), calls=%async_computation.4 | async-start | bytes 65536 | tf_op jit(solution)/shard_map/all_to_all | solution.py:100
  88.9 8.8 %all-to-all-start.5 = ((f32[4,1,1024]{2,1,0:T(1,128)}), f32[4,1,1024]{2,1,0:T(1,128)S(1)}, u32[]{:S(2)}, u32[]{:S(2)}) async-start(f32[4,1,1024]{2,1,0:T(1,128)} %reshape.1239), calls=%async_computation.5 | async-start | bytes 32768 | tf_op jit(solution)/shard_map/all_to_all | solution.py:96
  98.7 5.5 %collective-permute-start.6 = (f32[8,1,64]{2,1,0:T(1,128)S(1)}, f32[8,1,64]{2,1,0:T(1,128)S(1)}, u32[]{:S(2)}, u32[]{:S(2)}) collective-permute-start(f32[8,1,64]{2,1,0:T(1,128)S(1)} %get-tuple-element.22), channel_id=1, source_target_pairs={{0,8},{8,16},{16,24},{24,0},{1,9},{9,17},{17,25},{25,1},{2,10},{10... | collective-permute-start | bytes 6152 | tf_op jit(solution)/shard_map/ppermute | solution.py:26
  99.4 4.8 %collective-permute-start.7 = (f32[8,1,64]{2,1,0:T(1,128)S(1)}, f32[8,1,64]{2,1,0:T(1,128)S(1)}, u32[]{:S(2)}, u32[]{:S(2)}) collective-permute-start(f32[8,1,64]{2,1,0:T(1,128)S(1)} %get-tuple-element.23), channel_id=1, source_target_pairs={{8,0},{16,8},{24,16},{0,24},{9,1},{17,9},{25,17},{1,25},{10,2},{18... | collective-permute-start | bytes 6152 | tf_op jit(solution)/shard_map/ppermute | solution.py:28
  104.3 1.3 collective-permute-start.8
  104.4 1.4 collective-permute-start.9
  105.0 3.8 %collective-permute-start.2 = (f32[16,48,16]{2,0,1:T(8,128)S(1)}, f32[16,48,16]{2,0,1:T(8,128)S(1)}, u32[]{:S(2)}, u32[]{:S(2)}) collective-permute-start(f32[16,48,16]{2,0,1:T(8,128)S(1)} %get-tuple-element.4), channel_id=1, source_target_pairs={{0,4},{4,0},{1,5},{5,1},{2,6},{6,2},{3,7},{7,3},{8,12},{12,8},{9,1... | collective-permute-start | bytes 147464 | tf_op jit(solution)/shard_map/ppermute | solution.py:26
  105.2 3.6 %collective-permute-start.3 = (f32[16,48,16]{2,0,1:T(8,128)S(1)}, f32[16,48,16]{2,0,1:T(8,128)S(1)}, u32[]{:S(2)}, u32[]{:S(2)}) collective-permute-start(f32[16,48,16]{2,0,1:T(8,128)S(1)} %get-tuple-element.5), channel_id=1, source_target_pairs={{4,0},{0,4},{5,1},{1,5},{6,2},{2,6},{7,3},{3,7},{12,8},{8,12},{13,... | collective-permute-start | bytes 147464 | tf_op jit(solution)/shard_map/ppermute | solution.py:28
  105.8 6.3 %collective-permute-start.10 = (f32[1,10,66]{2,1,0:T(8,128)S(1)}, f32[1,10,66]{2,1,0:T(8,128)S(1)}, u32[]{:S(2)}, u32[]{:S(2)}) collective-permute-start(f32[1,10,66]{2,1,0:T(8,128)S(1)} %get-tuple-element.16), channel_id=1, source_target_pairs={{0,1},{1,2},{2,3},{3,0},{4,5},{5,6},{6,7},{7,4},{8,9},{9,10},{10,1... | collective-permute-start | bytes 7928 | tf_op jit(solution)/shard_map/ppermute | solution.py:26
  106.5 5.6 %collective-permute-start.11 = (f32[1,10,66]{2,1,0:T(8,128)S(1)}, f32[1,10,66]{2,1,0:T(8,128)S(1)}, u32[]{:S(2)}, u32[]{:S(2)}) collective-permute-start(f32[1,10,66]{2,1,0:T(8,128)S(1)} %get-tuple-element.17), channel_id=1, source_target_pairs={{1,0},{2,1},{3,2},{0,3},{5,4},{6,5},{7,6},{4,7},{9,8},{10,9},{11,1... | collective-permute-start | bytes 7928 | tf_op jit(solution)/shard_map/ppermute | solution.py:28
  109.2 21.4 %collective-permute-start.4 = (f32[16,48,160]{2,0,1:T(8,128)S(1)}, f32[16,48,160]{2,0,1:T(8,128)S(1)}, u32[]{:S(2)}, u32[]{:S(2)}) collective-permute-start(f32[16,48,160]{2,0,1:T(8,128)S(1)} %pad_maximum_fusion), channel_id=1, source_target_pairs={{0,1},{1,2},{2,3},{3,0},{4,5},{5,6},{6,7},{7,4},{8,9},{9,10},{10,1... | collective-permute-start | bytes 1474568 | tf_op jit(solution)/shard_map/ppermute | solution.py:26
  109.2 36.2 %collective-permute-start.5 = (f32[16,48,160]{2,0,1:T(8,128)S(1)}, f32[16,48,160]{2,0,1:T(8,128)S(1)}, u32[]{:S(2)}, u32[]{:S(2)}) collective-permute-start(f32[16,48,160]{2,0,1:T(8,128)S(1)} %pad_maximum_fusion), channel_id=1, source_target_pairs={{1,0},{2,1},{3,2},{0,3},{5,4},{6,5},{7,6},{4,7},{9,8},{10,9},{11,1... | collective-permute-start | bytes 1474568 | tf_op jit(solution)/shard_map/ppermute | solution.py:28
where the time goes:
time: 161 us
  waiting for transfers between devices  59.2 us (37%)
  starting transfers between devices  38.2 us (24%)
  matrix products  27 us (17%)
  local copies, waits for them, and re-layouts  19.1 us (12%)
  other arithmetic  13.8 us (9%)
  between operations  3.31 us (2%)
    ppermute x6, waiting for transfers between devices, extended_2(): lax.ppermute(tail, axis, [(i, (i + 1) % count) for i in range(count)])  17.9 us
    ppermute x6, waiting for transfers between devices, extended_2(): lax.ppermute(head, axis, [((i + 1) % count, i) for i in range(count)])  15 us
    ppermute x6, starting transfers between devices, extended_2(): lax.ppermute(head, axis, [((i + 1) % count, i) for i in range(count)])  11.4 us
    all_to_all x2, waiting for transfers between devices, swap_columns(): lax.all_to_all(payload, ('gx', 'gy'), split_axis=2, concat_axis=2, tiled=...  11.2 us
    reshape x1, local copies, waits for them, and re-layouts, long_range(): density.reshape(local_x, 2, local_y, 2, local_z, 2).mean(axis=(1, 3, 5))  10.5 us
    all_to_all x2, waiting for transfers between devices, swap_depth(): lax.all_to_all(payload, 'gz', split_axis=2, concat_axis=2, tiled=True)  9.45 us
    all_to_all x2, starting transfers between devices, swap_columns(): lax.all_to_all(payload, ('gx', 'gy'), split_axis=2, concat_axis=2, tiled=...  8.48 us
    all_to_all x2, starting transfers between devices, swap_depth(): lax.all_to_all(payload, 'gz', split_axis=2, concat_axis=2, tiled=True)  7.14 us
  transfers between devices with their start and end apart: 18, of which 10 were waited for; matrix products, arithmetic and copies ran while one was open for 27% of the time, Pallas kernels for 0%

commit v1 on v0

--- a/solution.py
+++ b/solution.py
@@ -1,6 +1,11 @@
+import functools
+
 import jax
 import jax.numpy as jnp
+import numpy as np
 from jax import lax
+from jax.experimental import pallas as pl
+from jax.experimental.pallas import tpu as pltpu
 from jax.sharding import PartitionSpec as P
 
 RADIUS = 15
@@ -201,7 +206,7 @@
     return (far_pot, far_x, far_y, far_z)
 
 
-def shards(density):
+def block_shards(density):
     size_x, size_y, size_z = density.shape
     padded = extended_2(density, (("gx", 1), ("gy", 2), ("gz", 0)), MARGIN)
     coarse_field = long_range(density)
@@ -213,7 +218,332 @@
     return (potential, forces)
 
 
+LANES = 128
+ROWS = 8
+NAMES = ("gx", "gy", "gz")
+
+
+def cas(length):
+    grid = np.outer(np.arange(length), np.arange(length)) % length
+    angles = 2.0 * np.pi * grid / length
+    return np.cos(angles) + np.sin(angles)
+
+
+def averaging(length):
+    out = np.zeros((length // 2, length))
+    cells = np.arange(length // 2)
+    out[cells, 2 * cells] = 0.5
+    out[cells, 2 * cells + 1] = 0.5
+    return out
+
+
+def interpolation(length):
+    half = length // 2
+    out = np.zeros((length, half))
+    cells = np.arange(half)
+    out[2 * cells, cells] += 0.75
+    out[2 * cells, (cells - 1) % half] += 0.25
+    out[2 * cells + 1, cells] += 0.75
+    out[2 * cells + 1, (cells + 1) % half] += 0.25
+    return out
+
+
+def slope_rows(values):
+    return -0.5 * (np.roll(values, -1, 0) - np.roll(values, 1, 0))
+
+
+def eigenvalues(length):
+    offsets = np.arange(-RADIUS, RADIUS + 1)
+    waves = np.cos(2.0 * np.pi * np.outer(np.arange(length), offsets) / length)
+    out = []
+    for fraction in FRACTIONS:
+        spread = RADIUS * fraction
+        norm = np.sqrt(np.sum(np.exp(-(offsets**2) / spread**2)))
+        out.append(waves @ (np.exp(-(offsets**2) / (2.0 * spread**2)) / norm))
+    return np.stack(out)
+
+
+def green_table(sizes):
+    waves = [4.0 * np.sin(np.pi * np.arange(m) / m) ** 2 for m in sizes]
+    edges = [np.arange(m) == m // 2 for m in sizes]
+    kappa = waves[0][:, None, None] + waves[1][None, :, None] + waves[2][None, None, :]
+    dropped = edges[0][:, None, None] | edges[1][None, :, None] | edges[2][None, None, :]
+    dropped[0, 0, 0] = True
+    green = AMPLITUDE * np.exp(-SMOOTHING * SMOOTHING * kappa) / (kappa + 1.0 / SCREEN**2)
+    return np.where(dropped, 0.0, green) / np.prod(sizes)
+
+
+def tables(dims, count, halves, pair):
+    nx, ny, nz = dims
+    wide = nx // count
+    hx, hy, hz = cas(nx), cas(ny), cas(nz)
+    cx, cy, cz = cas(nx // 2), cas(ny // 2), cas(nz // 2)
+    eye_h, eye_y, eye_k = np.eye(halves), np.eye(pair), np.eye(wide)
+    side = halves * pair * nx
+    out = {}
+    out["hz"] = hz
+    out["cz"] = (cz @ averaging(nz)).T
+    out["lx"] = np.einsum("ab,yw,dkx->daykbwx", eye_h, eye_y, hx.reshape(count, wide, nx)).reshape(
+        side, side
+    )
+    out["lxc"] = np.concatenate([cx @ averaging(nx) / pair] * pair, axis=1)
+    out["ly"] = np.einsum("ab,kl,qsy->akqsbyl", eye_h, eye_k, hy.reshape(ny, count, pair)).reshape(
+        side, side
+    )
+    out["lyc"] = cy
+    fine = interpolation(ny) @ cy
+    for name, level in (("value", hy), ("slope", slope_rows(hy))):
+        out["by_" + name] = np.einsum(
+            "ab,kl,syq->saykblq", eye_h, eye_k, level.reshape(count, pair, ny)
+        ).reshape(side, side)
+    level = np.zeros((count, ROWS, ny // 2))
+    level[:, :pair] = fine.reshape(count, pair, -1)
+    level[:, pair : 2 * pair] = slope_rows(fine).reshape(count, pair, -1)
+    out["byc"] = level.reshape(count * ROWS, -1)
+    out["bx"] = np.einsum("ab,yw,xdk->ayxdbwk", eye_h, eye_y, hx.reshape(nx, count, wide)).reshape(
+        side, side
+    )
+    back = np.zeros((2 * pair, nx, count, ROWS))
+    for row in range(2 * pair):
+        back[row, :, :, row] = interpolation(nx) @ cx
+    out["bxc"] = back.reshape(2 * pair * nx, count * ROWS)
+    out["bzc"] = (interpolation(nz) @ cz).T
+    ev_y, ev_z = eigenvalues(ny), eigenvalues(nz)
+    weights = np.array(WEIGHTS) / (nx * ny * nz)
+    plane = np.einsum("g,gy,gz->gyz", weights, ev_y, ev_z)
+    out["plane"] = plane.reshape(len(WEIGHTS), ny, halves, LANES).transpose(0, 2, 1, 3)
+    out["green"] = green_table((nx // 2, ny // 2, nz // 2))
+    scalars = eigenvalues(nx).T.reshape(-1).astype(np.float32)
+    return {k: np.asarray(v, np.float32) for k, v in out.items()}, scalars
+
+
+def dot(a, b):
+    return jnp.dot(a, b, precision=PRECISE, preferred_element_type=jnp.float32)
+
+
+def spectral_kernel(shape, names, *refs):
+    nx, ny, nz, gx, gy, gz = shape
+    group, count = gy * gz, gx * gy * gz
+    wide = nx // count
+    n = len(names)
+    data, scal = refs[0], refs[1]
+    hbm = dict(zip(names, refs[2 : 2 + n]))
+    out = refs[2 + n]
+    tab = dict(zip(names, refs[3 + n : 3 + 2 * n]))
+    (send_b, recv_a, recv_b, send_c, recv_c, send_d, recv_d, send_e, tab_sem, sems, semr) = refs[
+        3 + 2 * n :
+    ]
+    ix, iy, iz = lax.axis_index("gx"), lax.axis_index("gy"), lax.axis_index("gz")
+    mine = iz * gy + iy
+    me = ix * group + mine
+
+    def where(p):
+        return {"gx": p // group, "gy": p % gy, "gz": (p % group) // gy}
+
+    loads = {}
+    for i, name in enumerate(names):
+        source = hbm[name].at[me] if name == "green" else hbm[name]
+        loads[name] = pltpu.make_async_copy(source, tab[name], tab_sem.at[i])
+        loads[name].start()
+
+    barrier = pltpu.get_barrier_semaphore()
+
+    def greet(j, carry):
+        pl.semaphore_signal(
+            barrier, inc=1, device_id=where((me + j) % count), device_id_type=pl.DeviceIdType.MESH
+        )
+        return carry
+
+    lax.fori_loop(1, count, greet, 0)
+    pl.semaphore_wait(barrier, count - 1)
+
+    def remote(src, dst, slot, p):
+        return pltpu.make_async_remote_copy(
+            src_ref=src,
+            dst_ref=dst,
+            send_sem=sems.at[slot],
+            recv_sem=semr.at[slot],
+            device_id=where(p),
+            device_id_type=pl.DeviceIdType.MESH,
+        )
+
+    def group_exchange(base, source, target, own):
+        def to(j):
+            other = (mine + j) % group
+            return remote(source(other), target(mine), base + j, ix * group + other)
+
+        def arrived(j):
+            other = (mine + group - j) % group
+            return remote(source(other), target(other), base + j, ix * group + other)
+
+        for j in range(1, group):
+            to(j).start()
+        own()
+        for j in range(1, group):
+            arrived(j).wait_recv()
+        return lambda: [to(j).wait_send() for j in range(1, group)]
+
+    def full_exchange(parts):
+        def start(j, carry):
+            other = (me + j) % count
+            for base, source, target in parts:
+                remote(source.at[other], target.at[me], base + j, other).start()
+            return carry
+
+        def arrive(j, carry):
+            other = (me + count - j) % count
+            for base, source, target in parts:
+                remote(source.at[other], target.at[other], base + j, other).wait_recv()
+            return carry
+
+        def sent(j, carry):
+            other = (me + j) % count
+            for base, source, target in parts:
+                remote(source.at[other], target.at[me], base + j, other).wait_send()
+            return carry
+
+        lax.fori_loop(1, count, start, 0)
+        for base, source, target in parts:
+            target[me] = source[me]
+        lax.fori_loop(1, count, arrive, 0)
+        lax.fori_loop(1, count, sent, 0)
+
+    pair = recv_a.shape[1]
+    edge = recv_a.shape[3]
+
+    def keep_a():
+        recv_a[iy, :, iz] = data[pl.ds(mine * pair, pair)]
+
+    sent_a = group_exchange(
+        0,
+        lambda h: data.at[pl.ds(h * pair, pair)],
+        lambda h: recv_a.at[h % gy, :, h // gy],
+        keep_a,
+    )
+    for name in names:
+        loads[name].wait()
+    cells = jnp.concatenate(
+        [recv_a[h].reshape(pair * nx, LANES) for h in range(gy)], axis=1
+    )
+    along = dot(cells, tab["hz"][...])
+    along = jnp.concatenate([along[:, h * LANES : (h + 1) * LANES] for h in range(gy)], axis=0)
+    send_b[...] = dot(tab["lx"][...], along).reshape(send_b.shape)
+    send_c[:, 0, :] = dot(tab["lxc"][...], dot(cells, tab["cz"][...]))
+    base = group
+    full_exchange([(base, send_b, recv_b), (base + count, send_c, recv_c)])
+    base += 2 * count
+    spectrum = dot(tab["ly"][...], recv_b[...].reshape(count * ROWS, LANES))
+    blocks = []
+    for h in range(gy):
+        for k in range(wide):
+            row = h * wide + k
+            response = sum(
+                scal[(me * wide + k) * len(WEIGHTS) + g] * tab["plane"][g, h]
+                for g in range(len(WEIGHTS))
+            )
+            blocks.append(spectrum[row * ny : (row + 1) * ny] * response)
+    spectrum = jnp.concatenate(blocks, axis=0)
+    coarse = dot(tab["lyc"][...], recv_c[:, 0, :]) * tab["green"][...]
+    send_d[:, 0] = dot(tab["by_value"][...], spectrum).reshape(send_b.shape)
+    send_d[:, 1] = dot(tab["by_slope"][...], spectrum).reshape(send_b.shape)
+    send_d[:, 2] = dot(tab["byc"][...], coarse).reshape(send_b.shape)
+    full_exchange([(base, send_d, recv_d)])
+    base += count
+    fields = []
+    for f in range(2):
+        level = dot(tab["bx"][...], recv_d[:, f].reshape(count * ROWS, LANES))
+        size = pair * nx
+        fields.append(
+            jnp.concatenate([level[h * size : (h + 1) * size] for h in range(gy)], axis=1)
+        )
+    far = dot(tab["bxc"][...], recv_d[:, 2].reshape(count * ROWS, LANES))
+    both = dot(jnp.concatenate(fields, axis=0), tab["hz"][...]) + dot(far, tab["bzc"][...])
+    for y in range(pair):
+        pot = both[y * nx : (y + 1) * nx]
+        force_y = both[(pair + y) * nx : (pair + y + 1) * nx]
+        force_x = -0.5 * (pltpu.roll(pot, nx - 1, 0) - pltpu.roll(pot, 1, 0))
+        force_z = -0.5 * (pltpu.roll(pot, nz - 1, 1) - pltpu.roll(pot, 1, 1))
+        for f, field in enumerate((pot, force_x, force_y, force_z)):
+            for a in range(gz):
+                for b in range(gy):
+                    send_e[a * gy + b, f, y] = field[
+                        a * edge : (a + 1) * edge, b * LANES : (b + 1) * LANES
+                    ]
+
+    def keep_e():
+        out[:, pl.ds(mine * pair, pair)] = send_e[mine]
+
+    sent_e = group_exchange(
+        base,
+        lambda h: send_e.at[h],
+        lambda h: out.at[:, pl.ds(h * pair, pair)],
+        keep_e,
+    )
+    sent_a()
+    sent_e()
+
+
+def spectral_fits(shape, counts):
+    gx, gy, gz = counts
+    nx, ny, nz = shape
+    count = gx * gy * gz
+    if ny % (2 * count) or ny != nx or nx != 2 * count or min(shape) < 2 * RADIUS + 2:
+        return False
+    return nz == 2 * LANES and gy == 2 and nx % (8 * gz) == 0
+
+
+def spectral_shards(counts, density):
+    gx, gy, gz = counts
+    sx, sy, sz = density.shape
+    dims = (sx * gz, sy * gx, sz * gy)
+    count, group = gx * gy * gz, gy * gz
+    pair = sy // group
+    consts, scalars = tables(dims, count, gy, pair)
+    names = tuple(consts)
+    arrays = [consts[k] for k in names]
+    any_spec = pl.BlockSpec(memory_space=pl.ANY)
+    vmem = pl.BlockSpec(memory_space=pltpu.VMEM)
+    tile = (count, ROWS, LANES)
+    slots = 2 * group + 3 * count
+    scratch = [
+        pltpu.VMEM(a.shape[1:] if k == "green" else a.shape, jnp.float32)
+        for k, a in consts.items()
+    ]
+    scratch += [
+        pltpu.VMEM(tile, jnp.float32),
+        pltpu.VMEM((gy, pair, gz, sx, LANES), jnp.float32),
+        pltpu.VMEM(tile, jnp.float32),
+        pltpu.VMEM((count, 1, LANES), jnp.float32),
+        pltpu.VMEM((count, 1, LANES), jnp.float32),
+        pltpu.VMEM((count, 3, ROWS, LANES), jnp.float32),
+        pltpu.VMEM((count, 3, ROWS, LANES), jnp.float32),
+        pltpu.VMEM((group, 4, pair, sx, LANES), jnp.float32),
+        pltpu.SemaphoreType.DMA((len(names),)),
+        pltpu.SemaphoreType.DMA((slots,)),
+        pltpu.SemaphoreType.DMA((slots,)),
+    ]
+    fields = pl.pallas_call(
+        functools.partial(spectral_kernel, dims + (gx, gy, gz), names),
+        out_shape=jax.ShapeDtypeStruct((4, sy, sx, sz), jnp.float32),
+        in_specs=[vmem, pl.BlockSpec(memory_space=pltpu.SMEM)] + [any_spec] * len(names),
+        out_specs=vmem,
+        scratch_shapes=scratch,
+        compiler_params=pltpu.CompilerParams(collective_id=0, has_side_effects=True),
+    )(density.transpose(1, 0, 2), jnp.asarray(scalars), *[jnp.asarray(a) for a in arrays])
+    fields = fields.transpose(0, 2, 1, 3)
+    return (fields[0], fields[1:])
+
+
 def solution(mesh):
+    counts = tuple(mesh.shape[a] for a in NAMES)
+
+    def shards(density):
+        sx, sy, sz = density.shape
+        dims = (sx * counts[2], sy * counts[0], sz * counts[1])
+        if spectral_fits(dims, counts):
+            return spectral_shards(counts, density)
+        return block_shards(density)
+
     return jax.shard_map(
         shards,
         mesh=mesh,

time: 161 us -> 47.1 us (0.29)
  the two profiles are of different devices: /device:TPU:0 before, /device:TPU:9 now
where the time goes in v1:
time: 47.1 us; the launch traced here: 46.9 us
  Pallas kernels  41.1 us (87%)
  local copies, waits for them, and re-layouts  5.11 us (11%)
  between operations  0.64 us (1%)
    pallas_call x1, Pallas kernels, spectral_shards(): pl.pallas_call(functools.partial(spectral_kernel, dims + (gx, gy, gz), na...  41.1 us
    unnamed x3, local copies, waits for them, and re-layouts  3.17 us
    slice x1, local copies, waits for them, and re-layouts, spectral_shards(): return (fields[0], fields[1:])  1.02 us

profile of v1, /device:TPU:9, one launch (start us, length us, event | category | flops | bytes accessed | tf_op | source)
XLA Modules:
  0.0 46.9 jit_solution(3888527867208550306)
XLA Ops:
  0.6 1.6 %copy.22 = f32[16,16,128]{2,0,1:T(8,128)} copy(f32[16,16,128]{2,1,0:T(8,128)} %param.16) | data formatting | bytes 262144 | tf_op args[0]
  2.2 41.1 %shard_map.167 = f32[4,16,16,128]{3,2,1,0:T(8,128)} custom-call(f32[16,16,128]{2,1,0:T(8,128)} %bitcast.8, f32[192]{0:T(256)} %constant.30.clone.refs_1_, f32[256,256]{1,0:T(8,128)} %constant.31.clone.refs_2_, f32[256,128]{1,0:T(8,128)} %constant.32.clone.refs_3_, f32[256,256]{1,0:T(8,128)} %constant.33.clone.refs_4_, f32[32,128]{1,0:T(8,128)} %constant.34.clone.refs_5_, ...), custom_call_target="tpu_custom_call" | custom-call | tf_op jit(solution)/shard_map/pallas_call | solution.py:525
  43.4 0.9 %slice_bitcast_fusion = f32[16,16,128]{2,0,1:T(8,128)S(1)} fusion(f32[4,16,16,128]{3,1,2,0:T(8,128)} %bitcast.6), kind=kLoop, calls=%fused_computation | loop fusion | bytes 262144 | tf_op jit(solution)/shard_map/squeeze | solution.py:534
  44.3 1.0 %slice.9 = f32[3,16,16,128]{3,1,2,0:T(8,128)S(1)} slice(f32[4,16,16,128]{3,1,2,0:T(8,128)} %bitcast.7), slice={[1:4], [0:16], [0:16], [0:128]} | slice | bytes 786432 | tf_op jit(solution)/shard_map/slice | solution.py:534
  45.3 0.9 %copy.20 = f32[3,16,16,128]{3,2,1,0:T(8,128)} copy(f32[3,16,16,128]{3,1,2,0:T(8,128)S(1)} %slice.9) | data formatting | bytes 786432
  46.2 0.7 %copy.19 = f32[16,16,128]{2,1,0:T(8,128)} copy(f32[16,16,128]{2,0,1:T(8,128)S(1)} %slice_bitcast_fusion) | data formatting | bytes 262144

commit v2 on v1

--- a/solution.py
+++ b/solution.py
@@ -317,8 +317,20 @@
     return {k: np.asarray(v, np.float32) for k, v in out.items()}, scalars
 
 
+def halves_of(values):
+    high = values.astype(jnp.bfloat16)
+    return high, (values - high.astype(jnp.float32)).astype(jnp.bfloat16)
+
+
+SPLIT = ("hz", "cz", "lx", "lxc", "ly", "lyc", "by_value", "by_slope", "byc", "bx", "bxc", "bzc")
+
+
 def dot(a, b):
-    return jnp.dot(a, b, precision=PRECISE, preferred_element_type=jnp.float32)
+    a_high, a_low = a if isinstance(a, tuple) else halves_of(a)
+    b_high, b_low = b if isinstance(b, tuple) else halves_of(b)
+    out = jnp.dot(a_high, b_low, preferred_element_type=jnp.float32)
+    out = out + jnp.dot(a_low, b_high, preferred_element_type=jnp.float32)
+    return out + jnp.dot(a_high, b_high, preferred_element_type=jnp.float32)
 
 
 def spectral_kernel(shape, names, *refs):
@@ -328,17 +340,41 @@
     n = len(names)
     data, scal = refs[0], refs[1]
     hbm = dict(zip(names, refs[2 : 2 + n]))
-    out = refs[2 + n]
-    tab = dict(zip(names, refs[3 + n : 3 + 2 * n]))
-    (send_b, recv_a, recv_b, send_c, recv_c, send_d, recv_d, send_e, tab_sem, sems, semr) = refs[
-        3 + 2 * n :
-    ]
+    out_pot, out_force = refs[2 + n : 4 + n]
+    tab = dict(zip(names, refs[4 + n : 4 + 2 * n]))
+    (
+        turned,
+        send_b,
+        recv_a,
+        recv_b,
+        send_c,
+        recv_c,
+        send_d,
+        recv_d,
+        send_e,
+        recv_e,
+        tab_sem,
+        sems,
+        semr,
+    ) = refs[4 + 2 * n :]
     ix, iy, iz = lax.axis_index("gx"), lax.axis_index("gy"), lax.axis_index("gz")
     mine = iz * gy + iy
     me = ix * group + mine
+    pair = recv_a.shape[1]
+    edge = recv_a.shape[3]
 
     def where(p):
         return {"gx": p // group, "gy": p % gy, "gz": (p % group) // gy}
+
+    barrier = pltpu.get_barrier_semaphore()
+
+    def greet(j, carry):
+        pl.semaphore_signal(
+            barrier, inc=1, device_id=where((me + j) % count), device_id_type=pl.DeviceIdType.MESH
+        )
+        return carry
+
+    lax.fori_loop(1, count, greet, 0)
 
     loads = {}
     for i, name in enumerate(names):
@@ -346,15 +382,13 @@
         loads[name] = pltpu.make_async_copy(source, tab[name], tab_sem.at[i])
         loads[name].start()
 
-    barrier = pltpu.get_barrier_semaphore()
-
-    def greet(j, carry):
-        pl.semaphore_signal(
-            barrier, inc=1, device_id=where((me + j) % count), device_id_type=pl.DeviceIdType.MESH
-        )
-        return carry
-
-    lax.fori_loop(1, count, greet, 0)
+    def table(name):
+        if name in loads:
+            loads.pop(name).wait()
+        values = tab[name]
+        return (values[0], values[1]) if name in SPLIT else values
+
+    turned[...] = jnp.transpose(data[...], (1, 0, 2))
     pl.semaphore_wait(barrier, count - 1)
 
     def remote(src, dst, slot, p):
@@ -367,7 +401,7 @@
             device_id_type=pl.DeviceIdType.MESH,
         )
 
-    def group_exchange(base, source, target, own):
+    def group_exchange(base, source, target):
         def to(j):
             other = (mine + j) % group
             return remote(source(other), target(mine), base + j, ix * group + other)
@@ -378,109 +412,141 @@
 
         for j in range(1, group):
             to(j).start()
-        own()
-        for j in range(1, group):
-            arrived(j).wait_recv()
-        return lambda: [to(j).wait_send() for j in range(1, group)]
-
-    def full_exchange(parts):
+
+        def arrive():
+            for j in range(1, group):
+                arrived(j).wait_recv()
+
+        def sent():
+            for j in range(1, group):
+                to(j).wait_send()
+
+        return arrive, sent
+
+    def full_exchange(base, source, target):
         def start(j, carry):
             other = (me + j) % count
-            for base, source, target in parts:
-                remote(source.at[other], target.at[me], base + j, other).start()
+            remote(source(other), target(me), base + j, other).start()
             return carry
 
-        def arrive(j, carry):
+        def arrived(j, carry):
             other = (me + count - j) % count
-            for base, source, target in parts:
-                remote(source.at[other], target.at[other], base + j, other).wait_recv()
+            remote(source(other), target(other), base + j, other).wait_recv()
             return carry
 
-        def sent(j, carry):
+        def gone(j, carry):
             other = (me + j) % count
-            for base, source, target in parts:
-                remote(source.at[other], target.at[me], base + j, other).wait_send()
+            remote(source(other), target(me), base + j, other).wait_send()
             return carry
 
         lax.fori_loop(1, count, start, 0)
-        for base, source, target in parts:
-            target[me] = source[me]
-        lax.fori_loop(1, count, arrive, 0)
-        lax.fori_loop(1, count, sent, 0)
-
-    pair = recv_a.shape[1]
-    edge = recv_a.shape[3]
-
-    def keep_a():
-        recv_a[iy, :, iz] = data[pl.ds(mine * pair, pair)]
-
-    sent_a = group_exchange(
+        return lambda: lax.fori_loop(1, count, arrived, 0), lambda: lax.fori_loop(1, count, gone, 0)
+
+    pending = []
+    arrive, sent = group_exchange(
         0,
-        lambda h: data.at[pl.ds(h * pair, pair)],
+        lambda h: turned.at[pl.ds(h * pair, pair)],
         lambda h: recv_a.at[h % gy, :, h // gy],
-        keep_a,
-    )
-    for name in names:
-        loads[name].wait()
-    cells = jnp.concatenate(
-        [recv_a[h].reshape(pair * nx, LANES) for h in range(gy)], axis=1
-    )
-    along = dot(cells, tab["hz"][...])
+    )
+    pending.append(sent)
+    recv_a[iy, :, iz] = turned[pl.ds(mine * pair, pair)]
+    hz, cz, lx, lxc = table("hz"), table("cz"), table("lx"), table("lxc")
+    arrive()
+    cells = halves_of(
+        jnp.concatenate([recv_a[h].reshape(pair * nx, LANES) for h in range(gy)], axis=1)
+    )
+    along = dot(cells, hz)
     along = jnp.concatenate([along[:, h * LANES : (h + 1) * LANES] for h in range(gy)], axis=0)
-    send_b[...] = dot(tab["lx"][...], along).reshape(send_b.shape)
-    send_c[:, 0, :] = dot(tab["lxc"][...], dot(cells, tab["cz"][...]))
+    send_b[...] = dot(lx, along).reshape(send_b.shape)
     base = group
-    full_exchange([(base, send_b, recv_b), (base + count, send_c, recv_c)])
-    base += 2 * count
-    spectrum = dot(tab["ly"][...], recv_b[...].reshape(count * ROWS, LANES))
-    blocks = []
+    arrive_b, sent = full_exchange(base, lambda p: send_b.at[p], lambda p: recv_b.at[p])
+    pending.append(sent)
+    send_c[:, 0, :] = dot(lxc, dot(cells, cz))
+    base += count
+    arrive_c, sent = full_exchange(base, lambda p: send_c.at[p], lambda p: recv_c.at[p])
+    pending.append(sent)
+    base += count
+    recv_b[me] = send_b[me]
+    recv_c[me] = send_c[me]
+    plane = table("plane")
+    responses = []
     for h in range(gy):
         for k in range(wide):
-            row = h * wide + k
-            response = sum(
-                scal[(me * wide + k) * len(WEIGHTS) + g] * tab["plane"][g, h]
-                for g in range(len(WEIGHTS))
+            responses.append(
+                sum(
+                    scal[(me * wide + k) * len(WEIGHTS) + g] * plane[g, h]
+                    for g in range(len(WEIGHTS))
+                )
             )
-            blocks.append(spectrum[row * ny : (row + 1) * ny] * response)
-    spectrum = jnp.concatenate(blocks, axis=0)
-    coarse = dot(tab["lyc"][...], recv_c[:, 0, :]) * tab["green"][...]
-    send_d[:, 0] = dot(tab["by_value"][...], spectrum).reshape(send_b.shape)
-    send_d[:, 1] = dot(tab["by_slope"][...], spectrum).reshape(send_b.shape)
-    send_d[:, 2] = dot(tab["byc"][...], coarse).reshape(send_b.shape)
-    full_exchange([(base, send_d, recv_d)])
+    response = jnp.concatenate(responses, axis=0)
+    ly, lyc, green = table("ly"), table("lyc"), table("green")
+    by_value, by_slope, byc = table("by_value"), table("by_slope"), table("byc")
+    arrive_b()
+    spectrum = dot(ly, recv_b[...].reshape(count * ROWS, LANES)) * response
+    spectrum = halves_of(spectrum)
+    send_d[:, 0] = dot(by_value, spectrum).reshape(send_b.shape)
+    arrive_c()
+    coarse = dot(lyc, recv_c[:, 0, :]) * green[...]
+    send_d[:, 1] = dot(byc, coarse).reshape(send_b.shape)
+    arrive_d, sent = full_exchange(
+        base, lambda p: send_d.at[p, pl.ds(0, 2)], lambda p: recv_d.at[p, pl.ds(0, 2)]
+    )
+    pending.append(sent)
     base += count
-    fields = []
-    for f in range(2):
-        level = dot(tab["bx"][...], recv_d[:, f].reshape(count * ROWS, LANES))
-        size = pair * nx
-        fields.append(
-            jnp.concatenate([level[h * size : (h + 1) * size] for h in range(gy)], axis=1)
-        )
-    far = dot(tab["bxc"][...], recv_d[:, 2].reshape(count * ROWS, LANES))
-    both = dot(jnp.concatenate(fields, axis=0), tab["hz"][...]) + dot(far, tab["bzc"][...])
+    send_d[:, 2] = dot(by_slope, spectrum).reshape(send_b.shape)
+    arrive_s, sent = full_exchange(base, lambda p: send_d.at[p, 2], lambda p: recv_d.at[p, 2])
+    pending.append(sent)
+    base += count
+    recv_d[me] = send_d[me]
+    bx, bxc, bzc = table("bx"), table("bxc"), table("bzc")
+    size = pair * nx
+
+    def near_part(f):
+        level = dot(bx, recv_d[:, f].reshape(count * ROWS, LANES))
+        level = jnp.concatenate([level[h * size : (h + 1) * size] for h in range(gy)], axis=1)
+        return dot(level, hz)
+
+    def place(f, y, field):
+        for a in range(gz):
+            for b in range(gy):
+                send_e[a * gy + b, f, y] = field[
+                    a * edge : (a + 1) * edge, b * LANES : (b + 1) * LANES
+                ]
+
+    arrive_d()
+    far = dot(dot(bxc, recv_d[:, 1].reshape(count * ROWS, LANES)), bzc)
+    values = near_part(0) + far[:size]
     for y in range(pair):
-        pot = both[y * nx : (y + 1) * nx]
-        force_y = both[(pair + y) * nx : (pair + y + 1) * nx]
-        force_x = -0.5 * (pltpu.roll(pot, nx - 1, 0) - pltpu.roll(pot, 1, 0))
-        force_z = -0.5 * (pltpu.roll(pot, nz - 1, 1) - pltpu.roll(pot, 1, 1))
-        for f, field in enumerate((pot, force_x, force_y, force_z)):
-            for a in range(gz):
-                for b in range(gy):
-                    send_e[a * gy + b, f, y] = field[
-                        a * edge : (a + 1) * edge, b * LANES : (b + 1) * LANES
-                    ]
-
-    def keep_e():
-        out[:, pl.ds(mine * pair, pair)] = send_e[mine]
-
-    sent_e = group_exchange(
+        pot = values[y * nx : (y + 1) * nx]
+        place(0, y, pot)
+        place(1, y, -0.5 * (pltpu.roll(pot, nx - 1, 0) - pltpu.roll(pot, 1, 0)))
+        place(2, y, -0.5 * (pltpu.roll(pot, nz - 1, 1) - pltpu.roll(pot, 1, 1)))
+    arrive_v, sent = group_exchange(
         base,
-        lambda h: send_e.at[h],
-        lambda h: out.at[:, pl.ds(h * pair, pair)],
-        keep_e,
-    )
-    sent_a()
-    sent_e()
+        lambda h: send_e.at[h, pl.ds(0, 3)],
+        lambda h: recv_e.at[pl.ds(0, 3), pl.ds(h * pair, pair)],
+    )
+    pending.append(sent)
+    base += group
+    arrive_s()
+    slopes = near_part(2) + far[size:]
+    for y in range(pair):
+        place(3, y, slopes[y * nx : (y + 1) * nx])
+    arrive_y, sent = group_exchange(
+        base,
+        lambda h: send_e.at[h, 3],
+        lambda h: recv_e.at[3, pl.ds(h * pair, pair)],
+    )
+    pending.append(sent)
+    recv_e[:, pl.ds(mine * pair, pair)] = send_e[mine]
+    arrive_v()
+    out_pot[...] = jnp.transpose(recv_e[0], (1, 0, 2))
+    out_force[0] = jnp.transpose(recv_e[1], (1, 0, 2))
+    out_force[2] = jnp.transpose(recv_e[2], (1, 0, 2))
+    arrive_y()
+    out_force[1] = jnp.transpose(recv_e[3], (1, 0, 2))
+    for sent in pending:
+        sent()
 
 
 def spectral_fits(shape, counts):
@@ -500,16 +566,21 @@
     pair = sy // group
     consts, scalars = tables(dims, count, gy, pair)
     names = tuple(consts)
+    for name in SPLIT:
+        full = consts[name]
+        high = full.astype(jnp.bfloat16)
+        consts[name] = np.stack([high, (full - high.astype(np.float32)).astype(jnp.bfloat16)])
     arrays = [consts[k] for k in names]
     any_spec = pl.BlockSpec(memory_space=pl.ANY)
     vmem = pl.BlockSpec(memory_space=pltpu.VMEM)
     tile = (count, ROWS, LANES)
-    slots = 2 * group + 3 * count
+    slots = 3 * group + 4 * count
     scratch = [
-        pltpu.VMEM(a.shape[1:] if k == "green" else a.shape, jnp.float32)
+        pltpu.VMEM(a.shape[1:] if k == "green" else a.shape, a.dtype)
         for k, a in consts.items()
     ]
     scratch += [
+        pltpu.VMEM((sy, sx, sz), jnp.float32),
         pltpu.VMEM(tile, jnp.float32),
         pltpu.VMEM((gy, pair, gz, sx, LANES), jnp.float32),
         pltpu.VMEM(tile, jnp.float32),
@@ -518,20 +589,22 @@
         pltpu.VMEM((count, 3, ROWS, LANES), jnp.float32),
         pltpu.VMEM((count, 3, ROWS, LANES), jnp.float32),
         pltpu.VMEM((group, 4, pair, sx, LANES), jnp.float32),
+        pltpu.VMEM((4, sy, sx, LANES), jnp.float32),
         pltpu.SemaphoreType.DMA((len(names),)),
         pltpu.SemaphoreType.DMA((slots,)),
         pltpu.SemaphoreType.DMA((slots,)),
     ]
-    fields = pl.pallas_call(
+    return pl.pallas_call(
         functools.partial(spectral_kernel, dims + (gx, gy, gz), names),
-        out_shape=jax.ShapeDtypeStruct((4, sy, sx, sz), jnp.float32),
+        out_shape=(
+            jax.ShapeDtypeStruct((sx, sy, sz), jnp.float32),
+            jax.ShapeDtypeStruct((3, sx, sy, sz), jnp.float32),
+        ),
         in_specs=[vmem, pl.BlockSpec(memory_space=pltpu.SMEM)] + [any_spec] * len(names),
-        out_specs=vmem,
+        out_specs=(vmem, vmem),
         scratch_shapes=scratch,
         compiler_params=pltpu.CompilerParams(collective_id=0, has_side_effects=True),
-    )(density.transpose(1, 0, 2), jnp.asarray(scalars), *[jnp.asarray(a) for a in arrays])
-    fields = fields.transpose(0, 2, 1, 3)
-    return (fields[0], fields[1:])
+    )(density, jnp.asarray(scalars), *[jnp.asarray(a) for a in arrays])
 
 
 def solution(mesh):

time: 47.1 us -> 44.5 us (0.945)
  local copies, waits for them, and re-layouts: 5.11 us -> 3.33 us
  Pallas kernels: 41.1 us -> 40.3 us
    slice x1 -> x0, local copies, waits for them, and re-layouts: 1.02 us -> none  [spectral_shards(): return (fields[0], fields[1:])]
    squeeze x1 -> x0, local copies, waits for them, and re-layouts: 0.91 us -> none  [spectral_shards(): return (fields[0], fields[1:])]
    pallas_call x1, Pallas kernels: 41.1 us -> 40.3 us  [spectral_shards(): pl.pallas_call(functools.partial(spectral_kernel, dims + (gx, gy, gz), na...]
    unnamed x3 -> x2, local copies, waits for them, and re-layouts: 3.17 us -> 3.33 us
where the time goes in v2:
time: 44.5 us; the launch traced here: 44.3 us
  Pallas kernels  40.3 us (91%)
  local copies, waits for them, and re-layouts  3.33 us (7%)
  between operations  0.64 us (1%)
    pallas_call x1, Pallas kernels, spectral_shards(): pl.pallas_call(functools.partial(spectral_kernel, dims + (gx, gy, gz), na...  40.3 us
    unnamed x2, local copies, waits for them, and re-layouts  3.33 us

profile of v2, /device:TPU:9, one launch (start us, length us, event | category | flops | bytes accessed | tf_op | source)
XLA Modules:
  0.0 44.3 jit_solution(7102003664237679466)
XLA Ops:
  0.6 40.3 %shard_map.167 = (f32[16,16,128]{2,1,0:T(8,128)}, f32[3,16,16,128]{3,2,1,0:T(8,128)}) custom-call(f32[16,16,128]{2,1,0:T(8,128)} %refs_0_.1, f32[192]{0:T(256)} %constant.30.clone.refs_1_, bf16[2,256,256]{2,1,0:T(8,128)(2,1)} %constant.31.clone.refs_2_, bf16[2,256,128]{2,1,0:T(8,128)(2,1)} %constant.32.clone.refs_3_, ...), custom_call_target="tpu_custom_call" | custom-call | tf_op jit(solution)/shard_map/pallas_call | solution.py:597
  40.9 1.6 %copy.20 = f32[16,16,128]{2,1,0:T(8,128)} copy(f32[16,16,128]{2,1,0:T(8,128)} %get-tuple-element.4) | data formatting | bytes 262144
  42.5 1.8 %copy.21 = f32[3,16,16,128]{3,2,1,0:T(8,128)} copy(f32[3,16,16,128]{3,2,1,0:T(8,128)} %get-tuple-element.5) | data formatting | bytes 786432

commit v3 on v2

--- a/solution.py
+++ b/solution.py
@@ -338,10 +338,9 @@
     group, count = gy * gz, gx * gy * gz
     wide = nx // count
     n = len(names)
-    data, scal = refs[0], refs[1]
-    hbm = dict(zip(names, refs[2 : 2 + n]))
-    out_pot, out_force = refs[2 + n : 4 + n]
-    tab = dict(zip(names, refs[4 + n : 4 + 2 * n]))
+    hbm = dict(zip(names, refs[:n]))
+    recv_e = refs[n]
+    tab = dict(zip(names, refs[n + 1 : 2 * n + 1]))
     (
         turned,
         send_b,
@@ -351,12 +350,13 @@
         recv_c,
         send_d,
         recv_d,
+        send_s,
+        recv_s,
         send_e,
-        recv_e,
         tab_sem,
         sems,
         semr,
-    ) = refs[4 + 2 * n :]
+    ) = refs[2 * n + 1 :]
     ix, iy, iz = lax.axis_index("gx"), lax.axis_index("gy"), lax.axis_index("gz")
     mine = iz * gy + iy
     me = ix * group + mine
@@ -374,7 +374,7 @@
         )
         return carry
 
-    lax.fori_loop(1, count, greet, 0)
+    lax.fori_loop(1, count, greet, 0, unroll=True)
 
     loads = {}
     for i, name in enumerate(names):
@@ -388,7 +388,8 @@
         values = tab[name]
         return (values[0], values[1]) if name in SPLIT else values
 
-    turned[...] = jnp.transpose(data[...], (1, 0, 2))
+    scal = tab["scalars"]
+    turned[...] = jnp.transpose(table("density")[...], (1, 0, 2))
     pl.semaphore_wait(barrier, count - 1)
 
     def remote(src, dst, slot, p):
@@ -401,52 +402,31 @@
             device_id_type=pl.DeviceIdType.MESH,
         )
 
-    def group_exchange(base, source, target):
-        def to(j):
+    def group_exchange(slot, source, target, some_source, some_target):
+        for j in range(1, group):
             other = (mine + j) % group
-            return remote(source(other), target(mine), base + j, ix * group + other)
-
-        def arrived(j):
-            other = (mine + group - j) % group
-            return remote(source(other), target(other), base + j, ix * group + other)
-
-        for j in range(1, group):
-            to(j).start()
-
-        def arrive():
-            for j in range(1, group):
-                arrived(j).wait_recv()
-
-        def sent():
-            for j in range(1, group):
-                to(j).wait_send()
-
-        return arrive, sent
-
-    def full_exchange(base, source, target):
+            remote(source(other), target(mine), slot, ix * group + other).start()
+        total = remote(some_source, some_target, slot, ix * group + (mine + 1) % group)
+        return total.wait_recv, total.wait_send
+
+    def full_exchange(slot, source, target):
         def start(j, carry):
             other = (me + j) % count
-            remote(source(other), target(me), base + j, other).start()
+            remote(source.at[other], target.at[me], slot, other).start()
             return carry
 
-        def arrived(j, carry):
-            other = (me + count - j) % count
-            remote(source(other), target(other), base + j, other).wait_recv()
-            return carry
-
-        def gone(j, carry):
-            other = (me + j) % count
-            remote(source(other), target(me), base + j, other).wait_send()
-            return carry
-
-        lax.fori_loop(1, count, start, 0)
-        return lambda: lax.fori_loop(1, count, arrived, 0), lambda: lax.fori_loop(1, count, gone, 0)
+        lax.fori_loop(1, count, start, 0, unroll=True)
+        rest = pl.ds(0, count - 1)
+        total = remote(source.at[rest], target.at[rest], slot, (me + 1) % count)
+        return total.wait_recv, total.wait_send
 
     pending = []
     arrive, sent = group_exchange(
         0,
         lambda h: turned.at[pl.ds(h * pair, pair)],
         lambda h: recv_a.at[h % gy, :, h // gy],
+        turned.at[pl.ds(0, (group - 1) * pair)],
+        turned.at[pl.ds(0, (group - 1) * pair)],
     )
     pending.append(sent)
     recv_a[iy, :, iz] = turned[pl.ds(mine * pair, pair)]
@@ -458,16 +438,14 @@
     along = dot(cells, hz)
     along = jnp.concatenate([along[:, h * LANES : (h + 1) * LANES] for h in range(gy)], axis=0)
     send_b[...] = dot(lx, along).reshape(send_b.shape)
-    base = group
-    arrive_b, sent = full_exchange(base, lambda p: send_b.at[p], lambda p: recv_b.at[p])
+    arrive_b, sent = full_exchange(1, send_b, recv_b)
     pending.append(sent)
     send_c[:, 0, :] = dot(lxc, dot(cells, cz))
-    base += count
-    arrive_c, sent = full_exchange(base, lambda p: send_c.at[p], lambda p: recv_c.at[p])
+    arrive_c, sent = full_exchange(2, send_c, recv_c)
     pending.append(sent)
-    base += count
     recv_b[me] = send_b[me]
     recv_c[me] = send_c[me]
+    table("scalars")
     plane = table("plane")
     responses = []
     for h in range(gy):
@@ -488,21 +466,18 @@
     arrive_c()
     coarse = dot(lyc, recv_c[:, 0, :]) * green[...]
     send_d[:, 1] = dot(byc, coarse).reshape(send_b.shape)
-    arrive_d, sent = full_exchange(
-        base, lambda p: send_d.at[p, pl.ds(0, 2)], lambda p: recv_d.at[p, pl.ds(0, 2)]
-    )
+    arrive_d, sent = full_exchange(3, send_d, recv_d)
     pending.append(sent)
-    base += count
-    send_d[:, 2] = dot(by_slope, spectrum).reshape(send_b.shape)
-    arrive_s, sent = full_exchange(base, lambda p: send_d.at[p, 2], lambda p: recv_d.at[p, 2])
+    send_s[...] = dot(by_slope, spectrum).reshape(send_b.shape)
+    arrive_s, sent = full_exchange(4, send_s, recv_s)
     pending.append(sent)
-    base += count
     recv_d[me] = send_d[me]
+    recv_s[me] = send_s[me]
     bx, bxc, bzc = table("bx"), table("bxc"), table("bzc")
     size = pair * nx
 
-    def near_part(f):
-        level = dot(bx, recv_d[:, f].reshape(count * ROWS, LANES))
+    def near_part(received):
+        level = dot(bx, received.reshape(count * ROWS, LANES))
         level = jnp.concatenate([level[h * size : (h + 1) * size] for h in range(gy)], axis=1)
         return dot(level, hz)
 
@@ -515,38 +490,44 @@
 
     arrive_d()
     far = dot(dot(bxc, recv_d[:, 1].reshape(count * ROWS, LANES)), bzc)
-    values = near_part(0) + far[:size]
+    values = near_part(recv_d[:, 0]) + far[:size]
     for y in range(pair):
         pot = values[y * nx : (y + 1) * nx]
         place(0, y, pot)
         place(1, y, -0.5 * (pltpu.roll(pot, nx - 1, 0) - pltpu.roll(pot, 1, 0)))
         place(2, y, -0.5 * (pltpu.roll(pot, nz - 1, 1) - pltpu.roll(pot, 1, 1)))
     arrive_v, sent = group_exchange(
-        base,
+        5,
         lambda h: send_e.at[h, pl.ds(0, 3)],
         lambda h: recv_e.at[pl.ds(0, 3), pl.ds(h * pair, pair)],
+        send_e.at[pl.ds(0, group - 1), pl.ds(0, 3)],
+        send_e.at[pl.ds(0, group - 1), pl.ds(0, 3)],
     )
     pending.append(sent)
-    base += group
     arrive_s()
-    slopes = near_part(2) + far[size:]
+    slopes = near_part(recv_s[...]) + far[size:]
     for y in range(pair):
         place(3, y, slopes[y * nx : (y + 1) * nx])
     arrive_y, sent = group_exchange(
-        base,
+        6,
         lambda h: send_e.at[h, 3],
         lambda h: recv_e.at[3, pl.ds(h * pair, pair)],
+        send_e.at[pl.ds(0, group - 1), 3],
+        send_e.at[pl.ds(0, group - 1), 3],
     )
     pending.append(sent)
     recv_e[:, pl.ds(mine * pair, pair)] = send_e[mine]
     arrive_v()
-    out_pot[...] = jnp.transpose(recv_e[0], (1, 0, 2))
-    out_force[0] = jnp.transpose(recv_e[1], (1, 0, 2))
-    out_force[2] = jnp.transpose(recv_e[2], (1, 0, 2))
     arrive_y()
-    out_force[1] = jnp.transpose(recv_e[3], (1, 0, 2))
     for sent in pending:
         sent()
+
+
+def hand_out(fields, out_pot, out_force):
+    out_pot[...] = jnp.transpose(fields[0], (1, 0, 2))
+    out_force[0] = jnp.transpose(fields[1], (1, 0, 2))
+    out_force[1] = jnp.transpose(fields[3], (1, 0, 2))
+    out_force[2] = jnp.transpose(fields[2], (1, 0, 2))
 
 
 def spectral_fits(shape, counts):
@@ -565,20 +546,21 @@
     count, group = gx * gy * gz, gy * gz
     pair = sy // group
     consts, scalars = tables(dims, count, gy, pair)
-    names = tuple(consts)
     for name in SPLIT:
         full = consts[name]
         high = full.astype(jnp.bfloat16)
         consts[name] = np.stack([high, (full - high.astype(np.float32)).astype(jnp.bfloat16)])
-    arrays = [consts[k] for k in names]
+    scratch = {k: pltpu.VMEM(a.shape, a.dtype) for k, a in consts.items()}
+    scratch["green"] = pltpu.VMEM(consts["green"].shape[1:], jnp.float32)
+    scratch["density"] = pltpu.VMEM((sx, sy, sz), jnp.float32)
+    scratch["scalars"] = pltpu.SMEM(scalars.shape, jnp.float32)
+    given = {"density": density, "scalars": scalars, **consts}
+    names = tuple(given)
     any_spec = pl.BlockSpec(memory_space=pl.ANY)
     vmem = pl.BlockSpec(memory_space=pltpu.VMEM)
     tile = (count, ROWS, LANES)
-    slots = 3 * group + 4 * count
-    scratch = [
-        pltpu.VMEM(a.shape[1:] if k == "green" else a.shape, a.dtype)
-        for k, a in consts.items()
-    ]
+    slots = 7
+    scratch = [scratch[k] for k in names]
     scratch += [
         pltpu.VMEM((sy, sx, sz), jnp.float32),
         pltpu.VMEM(tile, jnp.float32),
@@ -586,25 +568,33 @@
         pltpu.VMEM(tile, jnp.float32),
         pltpu.VMEM((count, 1, LANES), jnp.float32),
         pltpu.VMEM((count, 1, LANES), jnp.float32),
-        pltpu.VMEM((count, 3, ROWS, LANES), jnp.float32),
-        pltpu.VMEM((count, 3, ROWS, LANES), jnp.float32),
+        pltpu.VMEM((count, 2, ROWS, LANES), jnp.float32),
+        pltpu.VMEM((count, 2, ROWS, LANES), jnp.float32),
+        pltpu.VMEM(tile, jnp.float32),
+        pltpu.VMEM(tile, jnp.float32),
         pltpu.VMEM((group, 4, pair, sx, LANES), jnp.float32),
-        pltpu.VMEM((4, sy, sx, LANES), jnp.float32),
         pltpu.SemaphoreType.DMA((len(names),)),
         pltpu.SemaphoreType.DMA((slots,)),
         pltpu.SemaphoreType.DMA((slots,)),
     ]
+    fields = pl.pallas_call(
+        functools.partial(spectral_kernel, dims + (gx, gy, gz), names),
+        out_shape=pltpu.VMEM((4, sy, sx, sz), jnp.float32),
+        in_specs=[any_spec] * len(names),
+        out_specs=vmem,
+        scratch_shapes=scratch,
+        compiler_params=pltpu.CompilerParams(collective_id=0, has_side_effects=True),
+    )(*[jnp.asarray(given[k]) for k in names])
+    fields = pltpu.with_memory_space_constraint(fields, pltpu.VMEM)
     return pl.pallas_call(
-        functools.partial(spectral_kernel, dims + (gx, gy, gz), names),
+        hand_out,
         out_shape=(
             jax.ShapeDtypeStruct((sx, sy, sz), jnp.float32),
             jax.ShapeDtypeStruct((3, sx, sy, sz), jnp.float32),
         ),
-        in_specs=[vmem, pl.BlockSpec(memory_space=pltpu.SMEM)] + [any_spec] * len(names),
+        in_specs=[vmem],
         out_specs=(vmem, vmem),
-        scratch_shapes=scratch,
-        compiler_params=pltpu.CompilerParams(collective_id=0, has_side_effects=True),
-    )(density, jnp.asarray(scalars), *[jnp.asarray(a) for a in arrays])
+    )(fields)
 
 
 def solution(mesh):

time: 44.5 us -> 36.2 us (0.81)
  Pallas kernels: 40.3 us -> 35.4 us
  local copies, waits for them, and re-layouts: 3.33 us -> 0 us
    pallas_call x1, Pallas kernels: 40.3 us -> 34.6 us  [spectral_shards(): pl.pallas_call(functools.partial(spectral_kernel, dims + (gx, gy, gz), na...]
    unnamed x2 -> x0, local copies, waits for them, and re-layouts: 3.33 us -> none
    pallas_call x0 -> x1, Pallas kernels: none -> 0.84 us  [spectral_shards(): pl.pallas_call(hand_out, out_shape=(jax.ShapeDtypeStruct((sx, sy, sz), jn...]
where the time goes in v3:
time: 36.2 us; the launch traced here: 36.1 us
  Pallas kernels  35.4 us (98%)
  between operations  0.64 us (2%)
    pallas_call x1, Pallas kernels, spectral_shards(): pl.pallas_call(functools.partial(spectral_kernel, dims + (gx, gy, gz), na...  34.6 us
    pallas_call x1, Pallas kernels, spectral_shards(): pl.pallas_call(hand_out, out_shape=(jax.ShapeDtypeStruct((sx, sy, sz), jn...  0.84 us

profile of v3, /device:TPU:9, one launch (start us, length us, event | category | flops | bytes accessed | tf_op | source)
XLA Modules:
  0.0 36.1 jit_solution(7029950490981924112)
XLA Ops:
  0.6 34.6 %shard_map.167.fields = f32[4,16,16,128]{3,2,1,0:T(8,128)S(1)} custom-call(f32[16,16,128]{2,1,0:T(8,128)} %refs_0_.1, f32[192]{0:T(256)} %constant.30.clone.refs_1_, bf16[2,256,256]{2,1,0:T(8,128)(2,1)} %constant.31.clone.refs_2_, bf16[2,256,128]{2,1,0:T(8,128)(2,1)} %constant.32.clone.refs_3_, bf16[2,256,256]{2,1,0:T(8,128)(2,1)} %constant.33.clone.refs_4_, ...), custom_call_target="tpu_custom_call" | custom-call | tf_op jit(solution)/shard_map/pallas_call | solution.py:580
  35.2 0.8 %shard_map.168 = (f32[16,16,128]{2,1,0:T(8,128)}, f32[3,16,16,128]{3,2,1,0:T(8,128)}) custom-call(f32[4,16,16,128]{3,2,1,0:T(8,128)S(1)} %shard_map.167.fields), custom_call_target="tpu_custom_call" | custom-call | tf_op jit(solution)/shard_map/pallas_call | solution.py:589

commit v4 on v3

--- a/solution.py
+++ b/solution.py
@@ -410,12 +410,11 @@
         return total.wait_recv, total.wait_send
 
     def full_exchange(slot, source, target):
-        def start(j, carry):
-            other = (me + j) % count
-            remote(source.at[other], target.at[me], slot, other).start()
-            return carry
-
-        lax.fori_loop(1, count, start, 0, unroll=True)
+        for k in sorted(range(gx), key=lambda k: -min(k, gx - k)):
+            for m in range(group):
+                if k or m:
+                    other = (ix + k) % gx * group + (mine + m) % group
+                    remote(source.at[other], target.at[me], slot, other).start()
         rest = pl.ds(0, count - 1)
         total = remote(source.at[rest], target.at[rest], slot, (me + 1) % count)
         return total.wait_recv, total.wait_send

time: 36.2 us -> 36.2 us (level)
  no operation moved by 1% of the time
where the time goes in v4:
time: 36.2 us; the launch traced here: 36.1 us
  Pallas kernels  35.4 us (98%)
  between operations  0.64 us (2%)
    pallas_call x1, Pallas kernels, spectral_shards(): pl.pallas_call(functools.partial(spectral_kernel, dims + (gx, gy, gz), na...  34.6 us
    pallas_call x1, Pallas kernels, spectral_shards(): pl.pallas_call(hand_out, out_shape=(jax.ShapeDtypeStruct((sx, sy, sz), jn...  0.84 us

profile of v4, /device:TPU:9, one launch (start us, length us, event | category | flops | bytes accessed | tf_op | source)
XLA Modules:
  0.0 36.1 jit_solution(5363564446497666853)
XLA Ops:
  0.6 34.6 %shard_map.167.fields = f32[4,16,16,128]{3,2,1,0:T(8,128)S(1)} custom-call(f32[16,16,128]{2,1,0:T(8,128)} %refs_0_.1, f32[192]{0:T(256)} %constant.30.clone.refs_1_, bf16[2,256,256]{2,1,0:T(8,128)(2,1)} %constant.31.clone.refs_2_, bf16[2,256,128]{2,1,0:T(8,128)(2,1)} %constant.32.clone.refs_3_, bf16[2,256,256]{2,1,0:T(8,128)(2,1)} %constant.33.clone.refs_4_, ...), custom_call_target="tpu_custom_call" | custom-call | tf_op jit(solution)/shard_map/pallas_call | solution.py:579
  35.2 0.8 %shard_map.168 = (f32[16,16,128]{2,1,0:T(8,128)}, f32[3,16,16,128]{3,2,1,0:T(8,128)}) custom-call(f32[4,16,16,128]{3,2,1,0:T(8,128)S(1)} %shard_map.167.fields), custom_call_target="tpu_custom_call" | custom-call | tf_op jit(solution)/shard_map/pallas_call | solution.py:588
